TPU v7x, 32 devices: a whole 2x2x4 slice. The times are simulated.
32 devices in a mesh: obs: 16 (over z, x, core), sp: 2 (over y).
Axes of the slice: x: 2, y: 2, z: 4, core: 2. Of those that a mesh axis runs over, the one named last changes fastest.
Arguments:
- descriptors: bfloat16 [16384, 512], P('obs'), may hold values from -10 to 10
- candidates: bfloat16 [8192, 512], P('obs'), may hold values from -10 to 10
- sparse_index: int32 [4096], replicated, may hold values from 0 to 8191, as said below
- targets: bfloat16 [16384], P('obs'), may hold values from -12 to 12
- regularizer: float32 [4096], replicated, may hold values from 0.25 to 1
Outputs:
- inverse: float32 [4096, 4096], P('sp', 'obs')
- weights: float32 [4096], P('sp')
Inputs may be any that keep to these rules, and one draw needn't show every extreme that they name: `sparse_index`: the 4096 indices are distinct.
All inputs are finite; a program needn't handle non-finite values.
Results may differ from a plain program's by a relative error of at most 0.012.
Values may be sent and summed in bfloat16 or wider, within the bound.
A program may use at most 128 MiB of HBM per device.

v0:
```python
import math

import jax
import jax.numpy as jnp
from jax import lax
from jax.sharding import PartitionSpec as P

epsilon = 1e-06


def unit_rows(row_block):
    values = row_block.astype(jnp.float32)
    return (values * lax.rsqrt(jnp.sum(values * values, axis=1, keepdims=True) + epsilon)).astype(
        jnp.bfloat16
    )


def kernel_block(normed, sparse):
    inner = lax.dot_general(
        normed, sparse, (((1,), (1,)), ((), ())), preferred_element_type=jnp.float32
    )
    scaled = inner * math.sqrt(normed.shape[1])
    squared = scaled * scaled
    return (squared * squared - 6.0 * squared + 3.0).astype(jnp.bfloat16)


def select_rows(candidate_units, wanted, cand_start):
    shifted = wanted - cand_start
    inside = (shifted >= 0) & (shifted < candidate_units.shape[0])
    picked = candidate_units[jnp.clip(shifted, 0, candidate_units.shape[0] - 1)].astype(jnp.float32)
    return picked * inside[:, None].astype(jnp.float32)


def first_iterate(system_part, row_scale, col_scale, on_diag):
    return (
        jnp.where(on_diag, 2.0 * row_scale[:, None], 0.0)
        - system_part * row_scale[:, None] * col_scale[None, :]
    )


def on_device(descriptors, candidates, sparse_index, targets, regularizer):
    obs_count = lax.axis_size("obs")
    sp_count = lax.axis_size("sp")
    obs_pos = lax.axis_index("obs")
    sp_pos = lax.axis_index("sp")
    sparse_count = sparse_index.shape[0]
    block_rows = sparse_count // sp_count
    tile_cols = sparse_count // obs_count
    rows_all = descriptors.shape[0] * obs_count
    normed = unit_rows(descriptors)
    candidate_units = unit_rows(candidates)
    cand_start = obs_pos * candidates.shape[0]
    all_sparse = lax.psum(
        select_rows(candidate_units, sparse_index, cand_start).astype(jnp.bfloat16), "obs"
    )
    full_kernel = kernel_block(normed, all_sparse)
    own_kernel = lax.dynamic_slice_in_dim(full_kernel, sp_pos * block_rows, block_rows, 1)
    gram_part = lax.psum_scatter(
        lax.dot_general(
            full_kernel, own_kernel, (((0,), (0,)), ((), ())), preferred_element_type=jnp.float32
        ),
        "obs",
        scatter_dimension=0,
        tiled=True,
    )
    weighted = jnp.dot(targets, own_kernel, preferred_element_type=jnp.float32)
    squares = jnp.sum(jnp.square(own_kernel.astype(jnp.float32)), axis=0)
    weighted, squares = lax.psum((weighted, squares), "obs")
    weighted, squares = (
        lax.all_gather(weighted, "sp", axis=0, tiled=True),
        lax.all_gather(squares, "sp", axis=0, tiled=True),
    )
    normalizer = 24.0 * rows_all
    projected = weighted / math.sqrt(normalizer)
    recip = 1.0 / (squares / normalizer + regularizer)
    row_ids = sp_pos * block_rows + lax.iota(jnp.int32, block_rows)
    col_ids = obs_pos * tile_cols + lax.iota(jnp.int32, tile_cols)
    all_ids = lax.iota(jnp.int32, sparse_count)
    on_diag = row_ids[:, None] == col_ids[None, :]
    reg_rows = lax.dynamic_slice_in_dim(regularizer, sp_pos * block_rows, block_rows)
    recip_rows = lax.dynamic_slice_in_dim(recip, sp_pos * block_rows, block_rows)
    recip_cols = lax.dynamic_slice_in_dim(recip, obs_pos * tile_cols, tile_cols)
    system_tile = gram_part.T / normalizer + jnp.where(on_diag, reg_rows[:, None], 0.0)
    highest = lax.Precision.HIGHEST
    system_full_rows = lax.all_gather(system_tile, "obs", axis=1, tiled=True)
    system_full_cols = lax.all_gather(system_tile, "sp", axis=0, tiled=True)
    first_rows = first_iterate(
        system_full_rows, recip_rows, recip, row_ids[:, None] == all_ids[None, :]
    )
    first_cols = first_iterate(
        system_full_cols, recip, recip_cols, all_ids[:, None] == col_ids[None, :]
    )
    product_tile = jnp.dot(system_full_rows, first_cols, precision=highest)
    product_full_cols = lax.all_gather(product_tile, "sp", axis=0, tiled=True)
    first_tile = first_iterate(system_tile, recip_rows, recip_cols, on_diag)
    inverse_tile = 2.0 * first_tile - jnp.dot(first_rows, product_full_cols, precision=highest)
    projected_cols = lax.dynamic_slice_in_dim(projected, obs_pos * tile_cols, tile_cols)
    weight_part = jnp.dot(inverse_tile, projected_cols, precision=highest)
    weights = lax.psum(weight_part, "obs")
    return (inverse_tile, weights)


def solution(mesh):
    in_specs = (P("obs", None), P("obs", None), P(), P("obs"), P())
    out_specs = (P("sp", "obs"), P("sp"))
    return jax.shard_map(
        on_device, mesh=mesh, in_specs=in_specs, out_specs=out_specs, check_vma=False
    )
```

profile of v0, /device:TPU:0, one launch (start us, length us, event | category | flops | bytes accessed | tf_op | source)
XLA Modules:
  0.0 954.2 jit_solution(15224427852561429307)
XLA Ops:
  7.2 0.0 all-reduce.3.cloned.1.call-start
  7.2 0.7 fusion.36
  7.9 0.7 and_convert_fusion
  8.7 1.2 fusion.32
  9.9 1.2 fusion.33
  11.1 17.3 %gather_fusion = bf16[4096,512]{1,0:T(8,128)(2,1)} fusion(bf16[512,512]{1,0:T(8,128)(2,1)S(1)} %fusion.33, s32[4096]{0:T(1024)S(1)} %fusion.36), kind=kCustom, calls=%fused_computation | custom fusion | bytes 8404992 | tf_op jit(solution)/shard_map/gather | solution.py:30
  28.4 4.0 multiply_convert_fusion
  32.5 0.0 copy-start.3
  32.5 0.0 all-reduce.3.cloned.1.call-update
  32.5 0.0 reduce-scatter.2.cloned.1.call-start
  32.6 1.1 copy-done.3
  33.7 0.3 fusion.22
  34.0 112.7 %all-reduce.3.cloned.1.call-done = bf16[4096,512]{1,0:T(8,128)(2,1)} async-done(((bf16[4096,512]{1,0:T(8,128)(2,1)}), bf16[4096,512]{1,0:T(8,128)(2,1)}) %all-reduce.3.cloned.1.call-update) | async-done | bytes 4194320 | tf_op jit(solution)/shard_map/psum | solution.py:53
  146.7 7.7 add_convert_fusion
  154.4 0.0 copy-start.2
  154.4 3.2 copy-done.2
  157.6 22.4 %fusion.17 = f32[4096,2048]{1,0:T(8,128)} fusion(bf16[1024,4096]{1,0:T(8,128)(2,1)S(1)} %add_convert_fusion, s32[]{:T(128)} %select_n.28), kind=kOutput, calls=%fused_computation.23 | convolution fusion | flops 17179869184 | bytes 46137348 | tf_op jit(solution)/shard_map/dot_general | solution.py:59
  180.0 0.0 dynamic-slice-start
  180.0 0.0 reduce-scatter.2.cloned.1.call-update
  180.1 0.0 all-gather.6.cloned.1.call-start
  180.1 0.0 copy-start.5
  180.2 331.7 %reduce-scatter.2.cloned.1.call-done = f32[256,2048]{1,0:T(8,128)} async-done(((f32[4096,2048]{1,0:T(8,128)}), f32[256,2048]{1,0:T(8,128)}) %reduce-scatter.2.cloned.1.call-update) | async-done | bytes 2097168 | tf_op jit(solution)/shard_map/reduce_scatter | solution.py:58
  511.9 0.0 dynamic-slice-done
  511.9 3.3 fusion.26
  515.1 0.0 all-gather.6.cloned.1.call-update
  515.2 0.0 all-gather.4.cloned.1.call-start
  515.2 0.5 all-gather.4.cloned.1.call-update
  515.7 0.0 all-gather.8.cloned.1.call-start
  515.8 0.0 copy-done.5
  515.8 0.0 copy-start.4
  515.8 3.1 multiply_reduce_fusion
  518.9 3.3 fusion.15
  522.2 59.2 %all-reduce = (f32[2048]{0:T(1024)S(1)}, f32[2048]{0:T(1024)S(1)}) all-reduce(f32[2048]{0:T(1024)S(1)} %multiply_reduce_fusion, f32[2048]{0:T(1024)S(1)} %bitcast.13), channel_id=1, replica_groups=mesh['obs'=16,'sp'=2] {'obs'}, use_global_device_ids=true, to_apply=%region_4.5 | all-reduce | flops 4096 | bytes 32768 | tf_op jit(solution)/shard_map/psum | solution.py:68
  581.3 4.4 all_gather.15
  585.7 0.0 copy-done.4
  585.7 0.1 dynamic_slice.18
  585.8 0.0 all-gather.6.cloned.1.call-done
  585.8 155.6 %all-gather.4.cloned.1.call-done = f32[2048,4096]{0,1:T(8,128)} async-done(((f32[2048,256]{0,1:T(8,128)}), f32[2048,4096]{0,1:T(8,128)}) %all-gather.4.cloned.1.call-update) | async-done | bytes 33554448 | tf_op jit(solution)/shard_map/all_gather | solution.py:85
  741.3 0.0 copy-start
  741.3 66.7 %fusion.10 = f32[2048,256]{1,0:T(8,128)} fusion(f32[2048,4096]{0,1:T(8,128)} %all-gather.4.cloned.1.call-done, f32[4096,256]{0,1:T(8,128)} %all-gather.6.cloned.1.call-done, f32[256]{0:T(256)S(1)} %dynamic_slice.18, f32[4096]{0:T(1024)S(1)} %get-tuple-element.11, f32[4096]{0:T(1024)S(1)} %get-tuple-element.10, s32[256]{0:T(256)S(1)} %iota_add_fusion.1), kind=kOutput, calls=%fused_computation.15 | convolution fusion | flops 25775046656 | bytes 39880704 | tf_op jit(solution)/shard_map/dot_general | solution.py:93
  808.1 0.0 all-gather.8.cloned.1.call-update
  808.1 4.4 all_gather.19
  812.5 0.1 dynamic-slice_multiply_fusion
  812.5 52.5 %all-gather.8.cloned.1.call-done = f32[4096,256]{1,0:T(8,128)} async-done(((f32[2048,256]{1,0:T(8,128)}), f32[4096,256]{1,0:T(8,128)}) %all-gather.8.cloned.1.call-update) | async-done | bytes 4194320 | tf_op jit(solution)/shard_map/all_gather | solution.py:94
  865.0 0.0 copy-done
  865.0 44.1 %fusion.19 = f32[2048,256]{0,1:T(8,128)} fusion(f32[4096,256]{1,0:T(8,128)} %all-gather.8.cloned.1.call-done, f32[2048,4096]{0,1:T(8,128)} %all-gather.4.cloned.1.call-done, f32[4096]{0:T(1024)S(1)} %get-tuple-element.11, f32[2048]{0:T(1024)S(1)} %get-tuple-element.9, f32[2048]{0:T(1024)S(1)} %get-tuple-element.8, s32[2048]{0:T(1024)S(1)} %iota_add_fusion, ...), kind=kOutput, calls=%fused_computation.25 | convolution fusion | flops 25815416832 | bytes 41986048 | tf_op jit(solution)/shard_map/dot_general | solution.py:96
  909.1 0.0 copy-start.1
  909.1 3.0 copy.10
  912.1 0.0 copy-done.1
  912.1 1.2 fusion.41
  913.3 34.2 %psum.31 = f32[2048]{0:T(1024)} all-reduce(f32[2048]{0:T(1024)S(1)} %bitcast.12), channel_id=1, replica_groups=mesh['obs'=16,'sp'=2] {'obs'}, use_global_device_ids=true, to_apply=%region_7.8 | all-reduce | flops 2048 | bytes 16384 | tf_op jit(solution)/shard_map/psum | solution.py:99
  (7 shorter events, 0.0 us)
Async XLA Ops:
  7.2 139.6 %all-reduce.3.cloned.1.call-start = ((), (), s32[]{:S(2)}) async-start(), calls=%async_computation.1 | async-start | bytes 8388608 | tf_op jit(solution)/shard_map/psum | solution.py:53
  32.5 1.2 copy-start.3
  32.5 479.4 %reduce-scatter.2.cloned.1.call-start = ((), (), s32[]{:S(2)}) async-start(), calls=%async_computation.2 | async-start | bytes 35651584 | tf_op jit(solution)/shard_map/reduce_scatter | solution.py:58
  154.4 3.2 copy-start.2
  180.0 331.8 %dynamic-slice-start = ((f32[4096]{0:T(1024)}, s32[]{:T(128)}), f32[2048]{0:T(1024)S(1)}, s32[]{:S(2)}) async-start(f32[4096]{0:T(1024)} %param.9, s32[]{:T(128)} %select_n.28), calls=%async_computation.6 | async-start | bytes 16896 | tf_op jit(solution)/shard_map/dynamic_slice | solution.py:80
  180.1 405.7 %all-gather.6.cloned.1.call-start = ((), (), s32[]{:S(2)}) async-start(), calls=%async_computation.4 | async-start | bytes 6291456 | tf_op jit(solution)/shard_map/all_gather | solution.py:86
  180.1 335.6 %copy-start.5 = (bf16[1024]{0:T(1024)(128)(2,1)S(1)}, bf16[1024]{0:T(1024)(128)(2,1)}, u32[]{:S(2)}) copy-start(bf16[1024]{0:T(1024)(128)(2,1)} %param.8) | copy-start | bytes 6148
  515.2 226.2 %all-gather.4.cloned.1.call-start = ((), (), s32[]{:S(2)}) async-start(), calls=%async_computation.3 | async-start | bytes 35651584 | tf_op jit(solution)/shard_map/all_gather | solution.py:85
  515.7 349.3 %all-gather.8.cloned.1.call-start = ((), (), s32[]{:S(2)}) async-start(), calls=%async_computation.5 | async-start | bytes 6291456 | tf_op jit(solution)/shard_map/all_gather | solution.py:94
  515.8 69.9 %copy-start.4 = (f32[4096]{0:T(1024)S(1)}, f32[4096]{0:T(1024)}, u32[]{:S(2)}) copy-start(f32[4096]{0:T(1024)} %param.9) | copy-start | bytes 49156
  741.3 123.7 %copy-start = (f32[2048,256]{0,1:T(8,128)S(1)}, f32[2048,256]{0,1:T(8,128)}, u32[]{:S(2)}) copy-start(f32[2048,256]{0,1:T(8,128)} %fusion.26) | copy-start | bytes 6291460
  909.1 3.0 copy-start.1
Sparse Core Ops, SparseCore 0:
  32.6 114.0 all-reduce.2
  180.2 331.6 reduce-scatter.1
  515.3 55.7 all-gather.5
  573.2 168.0 all-gather.3
  808.2 56.7 all-gather.7
where the time goes:
time: 963 us; the launch traced here: 954 us
  waiting for transfers between devices  653 us (68%)
  matrix products  145 us (15%)
  blocking collectives  102 us (11%)
  local copies, waits for them, and re-layouts  24.8 us (3%)
  other arithmetic  14.6 us (2%)
  between operations  14.1 us (1%)
    reduce_scatter x1, waiting for transfers between devices, on_device(): lax.psum_scatter(lax.dot_general(full_kernel, own_kernel, (((0,), (0,)),...  332 us
    all_gather x1, waiting for transfers between devices, on_device(): system_full_rows = lax.all_gather(system_tile, 'obs', axis=1, tiled=True)  156 us
    psum x1, waiting for transfers between devices, on_device(): lax.psum(select_rows(candidate_units, sparse_index, cand_start).astype(jn...  113 us
    dot_general x1, matrix products, on_device(): product_tile = jnp.dot(system_full_rows, first_cols, precision=highest)  66.7 us
    psum x1, blocking collectives, on_device(): weighted, squares = lax.psum((weighted, squares), 'obs')  59.2 us
    all_gather x1, waiting for transfers between devices, on_device(): product_full_cols = lax.all_gather(product_tile, 'sp', axis=0, tiled=True)  52.5 us
    dot_general x1, matrix products, on_device(): jnp.dot(first_rows, product_full_cols, precision=highest)  44.1 us
    psum x1, blocking collectives, on_device(): weights = lax.psum(weight_part, 'obs')  34.2 us
  transfers between devices with their start and end apart: 5, of which 4 were waited for; matrix products, arithmetic and copies ran while one was open for 1% of the time, Pallas kernels for 0%

commit v1 on v0

v1 whole, which is shorter than its diff:
```python
import functools
import math

import jax
import jax.numpy as jnp
from jax import lax
from jax.experimental import pallas as pl
from jax.experimental.pallas import tpu as pltpu
from jax.sharding import PartitionSpec as P

epsilon = 1e-06
LANES = 128
VMEM_BYTES = 58 * 2**20


def unit_rows(row_block):
    values = row_block.astype(jnp.float32)
    return (values * lax.rsqrt(jnp.sum(values * values, axis=1, keepdims=True) + epsilon)).astype(
        jnp.bfloat16
    )


def gram_body(blocks, tile, share, ext, root, s_ref, norm_ref, sp_ref, tgt_ref, gram_ref, ws_ref, kext):
    step = pl.program_id(0)
    width = blocks * tile

    @pl.when(step < blocks)
    def _():
        inner = lax.dot_general(
            norm_ref[...], sp_ref[...], (((1,), (1,)), ((), ())), preferred_element_type=jnp.float32
        )
        scaled = inner * root
        squared = scaled * scaled
        kb = ((squared - 6.0) * squared + 3.0).astype(jnp.bfloat16)
        kext[:, pl.ds(pl.multiple_of(step * tile, tile), tile)] = kb

        @pl.when(step < ext)
        def _():
            kext[:, pl.ds(pl.multiple_of(width + step * tile, tile), tile)] = kb

        kf = kb.astype(jnp.float32)
        weighted = jnp.dot(tgt_ref[...], kb, preferred_element_type=jnp.float32)
        ws_ref[0:1, :] = weighted[0:1, :]
        ws_ref[1:2, :] = jnp.sum(kf * kf, axis=0, keepdims=True)

    @pl.when(step >= blocks)
    def _():
        j = step - blocks
        cols = pl.ds(pl.multiple_of(j * tile, tile), tile)
        window = pl.ds(pl.multiple_of(j * tile + s_ref[0] * share, LANES), share)
        gram_ref[...] = lax.dot_general(
            kext[:, cols], kext[:, window], (((0,), (0,)), ((), ())), preferred_element_type=jnp.float32
        ).astype(jnp.bfloat16)


def gram_call(s_pos, normed, sparse, targets, blocks, tile, share, sp_count):
    rows, depth = normed.shape
    width = blocks * tile
    ext = -(-((blocks - 1) * tile + sp_count * share - width) // tile)
    last = blocks - 1
    return pl.pallas_call(
        functools.partial(gram_body, blocks, tile, share, ext, math.sqrt(depth)),
        grid_spec=pltpu.PrefetchScalarGridSpec(
            num_scalar_prefetch=1,
            grid=(2 * blocks,),
            in_specs=[
                pl.BlockSpec((rows, depth), lambda g, s: (0, 0)),
                pl.BlockSpec((tile, depth), lambda g, s: (jnp.minimum(g, last), 0)),
                pl.BlockSpec((16, rows), lambda g, s: (0, 0)),
            ],
            out_specs=[
                pl.BlockSpec((tile, share), lambda g, s: (jnp.maximum(g - blocks, 0), 0)),
                pl.BlockSpec((2, tile), lambda g, s: (0, jnp.minimum(g, last))),
            ],
            scratch_shapes=[pltpu.VMEM((rows, width + ext * tile), jnp.bfloat16)],
        ),
        out_shape=[
            jax.ShapeDtypeStruct((width, share), jnp.bfloat16),
            jax.ShapeDtypeStruct((2, width), jnp.float32),
        ],
        compiler_params=pltpu.CompilerParams(vmem_limit_bytes=VMEM_BYTES),
    )(s_pos, normed, sparse, jnp.broadcast_to(targets[None, :], (16, rows)))


def newton_body(
    blocks, tile, share, sp_count, chunk, block_rows,
    pos_ref, packed_ref, rcol_ref, rrow_ref, y_ref, inv_ref, w_ref, dense, prod,
):
    step = pl.program_id(0)
    width = blocks * tile
    half = blocks // 2
    p_steps = width // chunk
    my_cols = pl.ds(pl.multiple_of(pos_ref[1] * tile, tile), tile)

    @pl.when(step < blocks)
    def _():
        rows = pl.ds(pl.multiple_of(step * tile, tile), tile)
        for s in range(sp_count):
            for q in range(share // LANES):
                offset = s * share + q * LANES
                if offset >= (half + 1) * tile:
                    continue
                col = lax.rem(step * tile + offset, width)
                cols = pl.ds(pl.multiple_of(col, LANES), LANES)
                block = packed_ref[s * tile : (s + 1) * tile, q * LANES : (q + 1) * LANES]
                dense[rows, cols] = block
                if tile <= offset < half * tile:
                    dense[cols, rows] = block.T

    @pl.when((step >= blocks) & (step < blocks + p_steps))
    def _():
        rows = pl.ds(pl.multiple_of((step - blocks) * chunk, chunk), chunk)
        prod[rows, :] = jnp.dot(
            dense[rows, :], dense[:, my_cols], preferred_element_type=jnp.float32
        ).astype(jnp.bfloat16)

    @pl.when(step >= blocks + p_steps)
    def _():
        local = pl.multiple_of((step - blocks - p_steps) * chunk, chunk)
        start = pl.multiple_of(pos_ref[0] * block_rows + local, chunk)
        rows = pl.ds(start, chunk)
        cubic = jnp.dot(dense[rows, :], prod[...], preferred_element_type=jnp.float32)
        on_diag = (start + lax.broadcasted_iota(jnp.int32, (chunk, tile), 0)) == (
            pos_ref[1] * tile + lax.broadcasted_iota(jnp.int32, (chunk, tile), 1)
        )
        series = (
            jnp.where(on_diag, 1.0, 0.0)
            - dense[rows, my_cols].astype(jnp.float32)
            + prod[rows, :].astype(jnp.float32)
            - cubic
        )
        out = series * rcol_ref[rows, :] * rrow_ref[...]
        inv_ref[pl.ds(local, chunk), :] = out
        w_ref[:, pl.ds(local, chunk)] = lax.dot_general(
            y_ref[...], out, (((1,), (1,)), ((), ())),
            precision=lax.Precision.HIGHEST, preferred_element_type=jnp.float32,
        )


def newton_call(pos, packed, root_recip, rrow, y, blocks, tile, share, sp_count):
    width = blocks * tile
    block_rows = width // sp_count
    chunk = min(512, block_rows)
    grid = blocks + width // chunk + block_rows // chunk
    last = blocks - 1
    return pl.pallas_call(
        functools.partial(newton_body, blocks, tile, share, sp_count, chunk, block_rows),
        grid_spec=pltpu.PrefetchScalarGridSpec(
            num_scalar_prefetch=1,
            grid=(grid,),
            in_specs=[
                pl.BlockSpec((sp_count * tile, share), lambda g, p: (jnp.minimum(g, last), 0)),
                pl.BlockSpec((width, 1), lambda g, p: (0, 0)),
                pl.BlockSpec((1, tile), lambda g, p: (0, 0)),
                pl.BlockSpec((8, tile), lambda g, p: (0, 0)),
            ],
            out_specs=[
                pl.BlockSpec((block_rows, tile), lambda g, p: (0, 0)),
                pl.BlockSpec((8, block_rows), lambda g, p: (0, 0)),
            ],
            scratch_shapes=[
                pltpu.VMEM((width, width), jnp.bfloat16),
                pltpu.VMEM((width, tile), jnp.bfloat16),
            ],
        ),
        out_shape=[
            jax.ShapeDtypeStruct((block_rows, tile), jnp.float32),
            jax.ShapeDtypeStruct((8, block_rows), jnp.float32),
        ],
        compiler_params=pltpu.CompilerParams(vmem_limit_bytes=VMEM_BYTES),
    )(pos, packed, root_recip[:, None], rrow[None, :], jnp.broadcast_to(y[None, :], (8, tile)))


def on_device(descriptors, candidates, sparse_index, targets, regularizer):
    obs_count = lax.axis_size("obs")
    sp_count = lax.axis_size("sp")
    obs_pos = lax.axis_index("obs")
    sp_pos = lax.axis_index("sp")
    width = sparse_index.shape[0]
    tile = width // obs_count
    share = -(-((obs_count // 2 + 1) * tile) // (sp_count * LANES)) * LANES
    normalizer = 24.0 * descriptors.shape[0] * obs_count

    normed = unit_rows(descriptors)
    piece = candidates.shape[0] // sp_count
    own = lax.dynamic_slice_in_dim(candidates, sp_pos * piece, piece)
    table = lax.all_gather(unit_rows(own), ("obs", "sp"), axis=0, tiled=True)
    sparse = table.at[sparse_index].get(mode="promise_in_bounds")

    gram, sums = gram_call(
        sp_pos[None].astype(jnp.int32), normed, sparse, targets, obs_count, tile, share, sp_count
    )
    sums = lax.psum(sums, "obs")
    gram, sums = lax.optimization_barrier((gram, sums))
    part = lax.psum_scatter(gram, "obs", scatter_dimension=0, tiled=True)

    projected = sums[0] / math.sqrt(normalizer)
    root = lax.rsqrt(sums[1] / normalizer + regularizer)
    col_start = obs_pos * tile
    rrow = lax.dynamic_slice_in_dim(root, col_start, tile)
    window_start = col_start + sp_pos * share
    rwin = lax.dynamic_slice_in_dim(jnp.concatenate([root, root]), window_start, share)
    offset = sp_pos * share + lax.iota(jnp.int32, share)
    on_diag = lax.iota(jnp.int32, tile)[:, None] == offset[None, :]
    scaled = jnp.where(
        on_diag, 0.0, part.astype(jnp.float32) * (rrow[:, None] / normalizer) * rwin[None, :]
    ).astype(jnp.bfloat16)
    packed = lax.all_gather(scaled, ("obs", "sp"), axis=0, tiled=True)

    y = lax.dynamic_slice_in_dim(projected, col_start, tile)
    pos = jnp.stack([sp_pos, obs_pos]).astype(jnp.int32)
    inverse_tile, part_w = newton_call(
        pos, packed, root, rrow, y, obs_count, tile, share, sp_count
    )
    return inverse_tile, lax.psum(part_w[0], "obs")


def solution(mesh):
    in_specs = (P("obs", None), P("obs", None), P(), P("obs"), P())
    out_specs = (P("sp", "obs"), P("sp"))
    return jax.shard_map(
        on_device, mesh=mesh, in_specs=in_specs, out_specs=out_specs, check_vma=False
    )
```

time: 963 us -> 522 us (0.54)
  waiting for transfers between devices: 653 us -> 308 us
  matrix products: 145 us -> 0 us
  Pallas kernels: 0 us -> 70.2 us
    reduce_scatter x1, waiting for transfers between devices: 332 us -> 107 us  [on_device(): part = lax.psum_scatter(gram, 'obs', scatter_dimension=0, tiled=True)]
    dot_general x6 -> x0, matrix products: 145 us -> none  [the longest x1 66.7 us: on_device(): product_tile = jnp.dot(system_full_rows, first_cols, precision=highest)]
    psum x1 -> x0, waiting for transfers between devices: 113 us -> none  [on_device(): lax.psum(select_rows(candidate_units, sparse_index, cand_start).astype(jn...]
    pallas_call x0 -> x2, Pallas kernels: none -> 70.2 us  [the longest x1 38.8 us: newton_call(): pl.pallas_call(functools.partial(newton_body, blocks, tile, share, sp_cou...]
    all_gather x3 -> x2, waiting for transfers between devices: 208 us -> 202 us  [the longest x1 124 us: on_device(): packed = lax.all_gather(scaled, ('obs', 'sp'), axis=0, tiled=True)]
  transfers between devices with their start and end apart: 5 -> 3, of which waited for: 4 -> 3; matrix products, arithmetic and copies ran while one was open for 1% -> 1% of each run, Pallas kernels for 0% -> 0%
where the time goes in v1:
time: 522 us; the launch traced here: 521 us
  waiting for transfers between devices  308 us (59%)
  blocking collectives  93 us (18%)
  Pallas kernels  70.2 us (13%)
  local copies, waits for them, and re-layouts  26.5 us (5%)
  between operations  13.8 us (3%)
  other arithmetic  9.23 us (2%)
    all_gather x1, waiting for transfers between devices, on_device(): packed = lax.all_gather(scaled, ('obs', 'sp'), axis=0, tiled=True)  124 us
    reduce_scatter x1, waiting for transfers between devices, on_device(): part = lax.psum_scatter(gram, 'obs', scatter_dimension=0, tiled=True)  107 us
    all_gather x1, waiting for transfers between devices, on_device(): table = lax.all_gather(unit_rows(own), ('obs', 'sp'), axis=0, tiled=True)  78.2 us
    psum x1, blocking collectives, on_device(): sums = lax.psum(sums, 'obs')  60.1 us
    pallas_call x1, Pallas kernels, newton_call(): pl.pallas_call(functools.partial(newton_body, blocks, tile, share, sp_cou...  38.8 us
    psum x1, blocking collectives, on_device(): return (inverse_tile, lax.psum(part_w[0], 'obs'))  32.8 us
    pallas_call x1, Pallas kernels, gram_call(): pl.pallas_call(functools.partial(gram_body, blocks, tile, share, ext, mat...  31.4 us
    gather x1, local copies, waits for them, and re-layouts, on_device(): sparse = table.at[sparse_index].get(mode='promise_in_bounds')  21.9 us
  transfers between devices with their start and end apart: 3, of which 3 were waited for; matrix products, arithmetic and copies ran while one was open for 1% of the time, Pallas kernels for 0%

profile of v1, /device:TPU:0, one launch (start us, length us, event | category | flops | bytes accessed | tf_op | source)
XLA Modules:
  0.0 521.4 jit_solution(16781584224758852121)
XLA Ops:
  7.2 0.0 copy-start
  7.2 0.0 copy-start.2
  7.2 0.0 all-gather.3.cloned.1.call-start
  7.2 1.2 fusion.2
  8.4 1.8 fusion.3
  10.2 0.0 all-gather.3.cloned.1.call-update
  10.2 0.0 reduce-scatter.2.cloned.1.call-start
  10.3 1.5 fusion
  11.8 0.0 copy-done.2
  11.8 0.0 copy-done
  11.8 1.3 fusion.1.norm_ref
  13.1 0.0 copy-start.3
  13.1 78.2 %all-gather.3.cloned.1.call-done = bf16[8192,512]{1,0:T(8,128)(2,1)} async-done(((bf16[256,512]{1,0:T(8,128)(2,1)}), bf16[8192,512]{1,0:T(8,128)(2,1)}) %all-gather.3.cloned.1.call-update) | async-done | bytes 8388624 | tf_op jit(solution)/shard_map/all_gather | solution.py:187
  91.3 21.9 %gather_fusion = bf16[4096,512]{1,0:T(8,128)(2,1)} fusion(bf16[8192,512]{1,0:T(8,128)(2,1)} %all-gather.3.cloned.1.call-done, s32[4096]{0:T(1024)S(1)} %fusion.4), kind=kCustom, calls=%fused_computation | custom fusion | bytes 8404992 | tf_op jit(solution)/shard_map/gather | solution.py:188
  113.2 0.0 copy-done.3
  113.2 0.6 broadcast_in_dim.16.tgt_ref
  113.8 31.4 %shard_map.68 = (bf16[4096,1152]{1,0:T(8,128)(2,1)}, f32[2,4096]{1,0:T(2,128)}) custom-call(s32[1]{0:T(128)} %bitcast.s_ref, bf16[1024,512]{1,0:T(8,128)(2,1)} %fusion.1.norm_ref, bf16[4096,512]{1,0:T(8,128)(2,1)} %gather_fusion, bf16[16,1024]{1,0:T(8,128)(2,1)} %broadcast_in_dim.16.tgt_ref), custom_call_target="tpu_custom_call" | custom-call | tf_op jit(solution)/shard_map/pallas_call | solution.py:61
  145.2 60.1 %psum.14 = f32[2,4096]{1,0:T(2,128)S(1)} all-reduce(f32[2,4096]{1,0:T(2,128)} %get-tuple-element.9), channel_id=1, replica_groups=mesh['obs'=16,'sp'=2] {'obs'}, use_global_device_ids=true, to_apply=%region_2.0 | all-reduce | flops 8192 | bytes 65536 | tf_op jit(solution)/shard_map/psum | solution.py:193
  205.4 0.0 copy-start.1
  205.4 0.0 reduce-scatter.2.cloned.1.call-update
  205.4 0.0 all-gather.5.cloned.1.call-start
  205.5 0.6 copy-done.1
  206.1 0.6 broadcast_multiply_fusion
  206.7 0.1 fusion.5
  206.8 106.6 %reduce-scatter.2.cloned.1.call-done = bf16[256,1152]{1,0:T(8,128)(2,1)} async-done(((bf16[4096,1152]{1,0:T(8,128)(2,1)}), bf16[256,1152]{1,0:T(8,128)(2,1)}) %reduce-scatter.2.cloned.1.call-update) | async-done | bytes 589840 | tf_op jit(solution)/shard_map/reduce_scatter | solution.py:195
  313.4 2.2 select_convert_fusion
  315.6 0.0 all-gather.5.cloned.1.call-update
  315.6 0.6 pad_add_fusion.pos_ref
  316.2 2.0 copy.7.rcol_ref
  318.1 123.6 %all-gather.5.cloned.1.call-done.packed_ref = bf16[8192,1152]{1,0:T(8,128)(2,1)} async-done(((bf16[256,1152]{1,0:T(8,128)(2,1)}), bf16[8192,1152]{1,0:T(8,128)(2,1)}) %all-gather.5.cloned.1.call-update) | async-done | bytes 18874384 | tf_op jit(solution)/shard_map/all_gather | solution.py:208
  441.8 0.6 broadcast_in_dim.19.y_ref
  442.4 38.8 %shard_map.69 = (f32[2048,256]{1,0:T(8,128)}, f32[8,2048]{1,0:T(8,128)}) custom-call(s32[2]{0:T(128)} %pad_add_fusion.pos_ref, bf16[8192,1152]{1,0:T(8,128)(2,1)} %all-gather.5.cloned.1.call-done.packed_ref, f32[4096,1]{1,0:T(8,128)} %copy.7.rcol_ref, f32[1,256]{1,0:T(1,128)} %bitcast.10, f32[8,256]{1,0:T(8,128)} %broadcast_in_dim.19.y_ref), custom_call_target="tpu_custom_call" | custom-call | tf_op jit(solution)/shard_map/pallas_call | solution.py:146
  481.2 0.8 slice.11
  482.0 32.8 %psum.15 = f32[2048]{0:T(1024)} all-reduce(f32[2048]{0:T(1024)S(1)} %bitcast.9), channel_id=1, replica_groups=mesh['obs'=16,'sp'=2] {'obs'}, use_global_device_ids=true, to_apply=%region_4.5 | all-reduce | flops 2048 | bytes 16384 | tf_op jit(solution)/shard_map/psum | solution.py:215
  (7 shorter events, 0.1 us)
Async XLA Ops:
  7.2 4.6 copy-start
  7.2 4.6 copy-start.2
  7.2 84.1 %all-gather.3.cloned.1.call-start = ((), (), s32[]{:S(2)}) async-start(), calls=%async_computation.1 | async-start | bytes 8650752 | tf_op jit(solution)/shard_map/all_gather | solution.py:187
  10.2 303.2 %reduce-scatter.2.cloned.1.call-start = ((), (), s32[]{:S(2)}) async-start(), calls=%async_computation.2 | async-start | bytes 10027008 | tf_op jit(solution)/shard_map/reduce_scatter | solution.py:195
  13.1 100.1 %copy-start.3 = (bf16[1024]{0:T(1024)(128)(2,1)S(1)}, bf16[1024]{0:T(1024)(128)(2,1)}, u32[]{:S(2)}) copy-start(bf16[1024]{0:T(1024)(128)(2,1)} %param.8) | copy-start | bytes 6148
  205.4 0.7 copy-start.1
  205.4 236.4 %all-gather.5.cloned.1.call-start = ((), (), s32[]{:S(2)}) async-start(), calls=%async_computation.3 | async-start | bytes 19464192 | tf_op jit(solution)/shard_map/all_gather | solution.py:208
Sparse Core Ops, SparseCore 0:
  11.1 80.1 all-gather.2
  205.5 107.8 reduce-scatter.1
  317.3 124.4 all-gather.4

commit v2 on v1

--- a/solution.py
+++ b/solution.py
@@ -171,6 +171,56 @@
     )(pos, packed, root_recip[:, None], rrow[None, :], jnp.broadcast_to(y[None, :], (8, tile)))
 
 
+def add_body(count, in_ref, out_ref, slots, send_sem, recv_sem):
+    me = lax.axis_index("obs")
+    barrier = pltpu.get_barrier_semaphore()
+    for k in range(1, count):
+        pl.semaphore_signal(
+            barrier, inc=1, device_id={"obs": lax.rem(me + k, count)}, device_id_type=pl.DeviceIdType.MESH
+        )
+    pl.semaphore_wait(barrier, count - 1)
+    copies = []
+    for k in range(1, count):
+        copy = pltpu.make_async_remote_copy(
+            src_ref=in_ref,
+            dst_ref=slots.at[me],
+            send_sem=send_sem.at[k],
+            recv_sem=recv_sem.at[k],
+            device_id={"obs": lax.rem(me + k, count)},
+            device_id_type=pl.DeviceIdType.MESH,
+        )
+        copy.start()
+        copies.append(copy)
+    slots[me] = in_ref[...]
+    for copy in copies:
+        copy.wait()
+    total = slots[0]
+    for k in range(1, count):
+        total = total + slots[k]
+    out_ref[...] = total
+
+
+def add_over_obs(values, count, collective_id):
+    shape = values.shape
+    flat = values.reshape(values.size // LANES, LANES)
+    total = pl.pallas_call(
+        functools.partial(add_body, count),
+        out_shape=jax.ShapeDtypeStruct(flat.shape, flat.dtype),
+        in_specs=[pl.BlockSpec(memory_space=pltpu.VMEM)],
+        out_specs=pl.BlockSpec(memory_space=pltpu.VMEM),
+        scratch_shapes=[
+            pltpu.VMEM((count,) + flat.shape, flat.dtype),
+            pltpu.SemaphoreType.DMA((count,)),
+            pltpu.SemaphoreType.DMA((count,)),
+        ],
+        cost_estimate=pl.CostEstimate(
+            flops=count * flat.size, bytes_accessed=400 * flat.size, transcendentals=0
+        ),
+        compiler_params=pltpu.CompilerParams(collective_id=collective_id, has_side_effects=True),
+    )(flat)
+    return total.reshape(shape)
+
+
 def on_device(descriptors, candidates, sparse_index, targets, regularizer):
     obs_count = lax.axis_size("obs")
     sp_count = lax.axis_size("sp")
@@ -182,16 +232,13 @@
     normalizer = 24.0 * descriptors.shape[0] * obs_count
 
     normed = unit_rows(descriptors)
-    piece = candidates.shape[0] // sp_count
-    own = lax.dynamic_slice_in_dim(candidates, sp_pos * piece, piece)
-    table = lax.all_gather(unit_rows(own), ("obs", "sp"), axis=0, tiled=True)
+    table = lax.all_gather(unit_rows(candidates), "obs", axis=0, tiled=True)
     sparse = table.at[sparse_index].get(mode="promise_in_bounds")
 
     gram, sums = gram_call(
         sp_pos[None].astype(jnp.int32), normed, sparse, targets, obs_count, tile, share, sp_count
     )
-    sums = lax.psum(sums, "obs")
-    gram, sums = lax.optimization_barrier((gram, sums))
+    sums = add_over_obs(sums, obs_count, 0)
     part = lax.psum_scatter(gram, "obs", scatter_dimension=0, tiled=True)
 
     projected = sums[0] / math.sqrt(normalizer)
@@ -212,7 +259,7 @@
     inverse_tile, part_w = newton_call(
         pos, packed, root, rrow, y, obs_count, tile, share, sp_count
     )
-    return inverse_tile, lax.psum(part_w[0], "obs")
+    return inverse_tile, add_over_obs(part_w[0], obs_count, 1)
 
 
 def solution(mesh):

time: 522 us -> 439 us (0.84)
  blocking collectives: 93 us -> 0 us
  Pallas kernels: 70.2 us -> 91.7 us
  waiting for transfers between devices: 308 us -> 293 us
    psum x2 -> x0, blocking collectives: 93 us -> none  [the longest x1 60.1 us: on_device(): sums = lax.psum(sums, 'obs')]
    pallas_call x0 -> x2, Pallas kernels: none -> 21.5 us  [add_over_obs(): pl.pallas_call(functools.partial(add_body, count), out_shape=jax.ShapeDty...]
    reduce_scatter x1, waiting for transfers between devices: 107 us -> 93.8 us  [on_device(): part = lax.psum_scatter(gram, 'obs', scatter_dimension=0, tiled=True)]
  transfers between devices with their start and end apart: 3 -> 3, of which waited for: 3 -> 3; matrix products, arithmetic and copies ran while one was open for 1% -> 2% of each run, Pallas kernels for 0% -> 3%
where the time goes in v2:
time: 439 us; the launch traced here: 438 us
  waiting for transfers between devices  293 us (67%)
  Pallas kernels  91.7 us (21%)
  local copies, waits for them, and re-layouts  29.2 us (7%)
  between operations  13.9 us (3%)
  other arithmetic  9.81 us (2%)
    all_gather x1, waiting for transfers between devices, on_device(): packed = lax.all_gather(scaled, ('obs', 'sp'), axis=0, tiled=True)  123 us
    reduce_scatter x1, waiting for transfers between devices, on_device(): part = lax.psum_scatter(gram, 'obs', scatter_dimension=0, tiled=True)  93.8 us
    all_gather x1, waiting for transfers between devices, on_device(): table = lax.all_gather(unit_rows(candidates), 'obs', axis=0, tiled=True)  76.1 us
    pallas_call x1, Pallas kernels, newton_call(): pl.pallas_call(functools.partial(newton_body, blocks, tile, share, sp_cou...  38.8 us
    pallas_call x1, Pallas kernels, gram_call(): pl.pallas_call(functools.partial(gram_body, blocks, tile, share, ext, mat...  31.4 us
    gather x1, local copies, waits for them, and re-layouts, on_device(): sparse = table.at[sparse_index].get(mode='promise_in_bounds')  21.9 us
    pallas_call x2, Pallas kernels, add_over_obs(): pl.pallas_call(functools.partial(add_body, count), out_shape=jax.ShapeDty...  21.5 us
  transfers between devices with their start and end apart: 3, of which 3 were waited for; matrix products, arithmetic and copies ran while one was open for 2% of the time, Pallas kernels for 3%

profile of v2, /device:TPU:0, one launch (start us, length us, event | category | flops | bytes accessed | tf_op | source)
XLA Modules:
  0.0 437.5 jit_solution(9696914945020315350)
XLA Ops:
  7.2 0.0 copy-start
  7.2 0.0 copy-start.3
  7.2 0.0 all-gather.3.cloned.1.call-start
  7.2 1.3 fusion.2
  8.5 2.0 fusion.3
  10.6 0.0 all-gather.3.cloned.1.call-update
  10.6 0.0 reduce-scatter.2.cloned.1.call-start
  10.7 0.0 copy-done
  10.7 0.3 fusion
  11.0 0.0 copy-done.3
  11.0 1.3 fusion.1.norm_ref
  12.2 0.0 copy-start.4
  12.2 76.1 %all-gather.3.cloned.1.call-done = bf16[8192,512]{1,0:T(8,128)(2,1)} async-done(((bf16[512,512]{1,0:T(8,128)(2,1)}), bf16[8192,512]{1,0:T(8,128)(2,1)}) %all-gather.3.cloned.1.call-update) | async-done | bytes 8388624 | tf_op jit(solution)/shard_map/all_gather | solution.py:235
  88.3 21.9 %gather_fusion = bf16[4096,512]{1,0:T(8,128)(2,1)} fusion(bf16[8192,512]{1,0:T(8,128)(2,1)} %all-gather.3.cloned.1.call-done, s32[4096]{0:T(1024)S(1)} %fusion.4), kind=kCustom, calls=%fused_computation | custom fusion | bytes 8404992 | tf_op jit(solution)/shard_map/gather | solution.py:236
  110.3 0.0 copy-done.4
  110.3 0.6 broadcast_in_dim.16.tgt_ref
  110.9 31.4 %shard_map.68 = (bf16[4096,1152]{1,0:T(8,128)(2,1)}, f32[2,4096]{1,0:T(2,128)}) custom-call(s32[1]{0:T(128)} %bitcast.s_ref, bf16[1024,512]{1,0:T(8,128)(2,1)} %fusion.1.norm_ref, bf16[4096,512]{1,0:T(8,128)(2,1)} %gather_fusion, bf16[16,1024]{1,0:T(8,128)(2,1)} %broadcast_in_dim.16.tgt_ref), custom_call_target="tpu_custom_call" | custom-call | tf_op jit(solution)/shard_map/pallas_call | solution.py:61
  142.3 0.0 copy-start.1
  142.3 0.0 copy-start.2
  142.3 0.0 reduce-scatter.2.cloned.1.call-update
  142.3 0.0 all-gather.5.cloned.1.call-start
  142.4 0.7 copy-done.1
  143.0 0.6 reshape.40.in_ref
  143.7 13.2 %shard_map.69 = f32[64,128]{1,0:T(8,128)} custom-call(f32[64,128]{1,0:T(8,128)} %reshape.40.in_ref), custom_call_target="tpu_custom_call" | custom-call | flops 131072 | bytes 3276800 | tf_op jit(solution)/shard_map/pallas_call | solution.py:206
  156.9 0.0 copy-done.2
  156.9 0.7 fusion.5
  157.6 0.7 broadcast_multiply_fusion
  158.3 0.1 fusion.6
  158.4 93.8 %reduce-scatter.2.cloned.1.call-done = bf16[256,1152]{1,0:T(8,128)(2,1)} async-done(((bf16[4096,1152]{1,0:T(8,128)(2,1)}), bf16[256,1152]{1,0:T(8,128)(2,1)}) %reduce-scatter.2.cloned.1.call-update) | async-done | bytes 589840 | tf_op jit(solution)/shard_map/reduce_scatter | solution.py:242
  252.2 2.2 select_convert_fusion
  254.3 0.0 all-gather.5.cloned.1.call-update
  254.4 0.6 pad_add_fusion.pos_ref
  254.9 0.7 multiply_bitcast_fusion
  255.6 0.1 dynamic_slice.11
  255.7 1.9 copy.7.rcol_ref
  257.7 122.9 %all-gather.5.cloned.1.call-done.packed_ref = bf16[8192,1152]{1,0:T(8,128)(2,1)} async-done(((bf16[256,1152]{1,0:T(8,128)(2,1)}), bf16[8192,1152]{1,0:T(8,128)(2,1)}) %all-gather.5.cloned.1.call-update) | async-done | bytes 18874384 | tf_op jit(solution)/shard_map/all_gather | solution.py:255
  380.5 0.6 broadcast_in_dim.19.y_ref
  381.1 38.8 %shard_map.70 = (f32[2048,256]{1,0:T(8,128)}, f32[8,2048]{1,0:T(8,128)}) custom-call(s32[2]{0:T(128)} %pad_add_fusion.pos_ref, bf16[8192,1152]{1,0:T(8,128)(2,1)} %all-gather.5.cloned.1.call-done.packed_ref, f32[4096,1]{1,0:T(8,128)} %copy.7.rcol_ref, f32[1,256]{1,0:T(1,128)} %bitcast.15, f32[8,256]{1,0:T(8,128)} %broadcast_in_dim.19.y_ref), custom_call_target="tpu_custom_call" | custom-call | tf_op jit(solution)/shard_map/pallas_call | solution.py:146
  419.9 1.4 slice.13
  421.4 8.3 %shard_map.71 = f32[16,128]{1,0:T(8,128)} custom-call(f32[16,128]{1,0:T(8,128)} %bitcast.14), custom_call_target="tpu_custom_call" | custom-call | flops 32768 | bytes 819200 | tf_op jit(solution)/shard_map/pallas_call | solution.py:206
  429.7 1.3 copy.9
  (4 shorter events, 0.0 us)
Async XLA Ops:
  7.2 3.5 copy-start
  7.2 3.8 copy-start.3
  7.2 81.2 %all-gather.3.cloned.1.call-start = ((), (), s32[]{:S(2)}) async-start(), calls=%async_computation.1 | async-start | bytes 8912896 | tf_op jit(solution)/shard_map/all_gather | solution.py:235
  10.6 241.6 %reduce-scatter.2.cloned.1.call-start = ((), (), s32[]{:S(2)}) async-start(), calls=%async_computation.2 | async-start | bytes 10027008 | tf_op jit(solution)/shard_map/reduce_scatter | solution.py:242
  12.2 98.0 %copy-start.4 = (bf16[1024]{0:T(1024)(128)(2,1)S(1)}, bf16[1024]{0:T(1024)(128)(2,1)}, u32[]{:S(2)}) copy-start(bf16[1024]{0:T(1024)(128)(2,1)} %param.8) | copy-start | bytes 6148
  142.3 0.8 copy-start.1
  142.3 14.6 %copy-start.2 = (f32[4096]{0:T(1024)S(1)}, f32[4096]{0:T(1024)}, u32[]{:S(2)}) copy-start(f32[4096]{0:T(1024)} %param.9) | copy-start | bytes 49156
  142.3 238.2 %all-gather.5.cloned.1.call-start = ((), (), s32[]{:S(2)}) async-start(), calls=%async_computation.3 | async-start | bytes 19464192 | tf_op jit(solution)/shard_map/all_gather | solution.py:255
Sparse Core Ops, SparseCore 0:
  10.7 77.5 all-gather.2
  142.4 109.6 reduce-scatter.1
  256.1 124.3 all-gather.4

commit v3 on v2

--- a/solution.py
+++ b/solution.py
@@ -221,6 +221,130 @@
     return total.reshape(shape)
 
 
+def spread_keys(z_count, sp_count):
+    keys = [("z", k) for k in range(1, z_count)]
+    for k in range(z_count):
+        keys += [("x", k), ("core", k), ("core_x", k)]
+        for d in range(1, sp_count):
+            keys += [(name, k, d) for name in ("sp", "sp_a", "x_b", "core_sp", "core_a", "core_b")]
+    return {key: place for place, key in enumerate(keys)}
+
+
+def spread_body(z_count, sp_count, in_ref, out_ref, send_sem, recv_sem, own_sem):
+    places = spread_keys(z_count, sp_count)
+    obs = lax.axis_index("obs")
+    s = lax.axis_index("sp")
+    z, x, c = lax.div(obs, 4), lax.rem(lax.div(obs, 2), 2), lax.rem(obs, 2)
+    half = in_ref.shape[0] // 2
+    upper, lower = pl.ds(0, half), pl.ds(half, half)
+    zs = [lax.bitwise_xor(z, k) for k in range(z_count)]
+    to_sp = [lax.rem(s + d, sp_count) for d in range(sp_count)]
+    from_sp = [lax.rem(s - d + sp_count, sp_count) for d in range(sp_count)]
+
+    def device(z_to, x_to, c_to, s_to):
+        return {"obs": z_to * 4 + x_to * 2 + c_to, "sp": s_to}
+
+    def slot(z_of, x_of, s_of):
+        return ((z_of * 2 + x_of) * 2 + c) * sp_count + s_of
+
+    own_slot = slot(z, x, s)
+    across, sibling = device(z, 1 - x, c, s), device(z, x, 1 - c, s)
+    others = [device(zs[k], x, c, s) for k in range(1, z_count)]
+    others += [device(z, x, c, to_sp[d]) for d in range(1, sp_count)]
+    others += [across, sibling]
+    barrier = pltpu.get_barrier_semaphore()
+    for other in others:
+        pl.semaphore_signal(barrier, inc=1, device_id=other, device_id_type=pl.DeviceIdType.MESH)
+    pl.semaphore_wait(barrier, len(others))
+
+    sent = {}
+
+    def send(key, place, target, rows=None, own=False):
+        src = in_ref if own else out_ref.at[place]
+        dst = out_ref.at[place]
+        if rows is not None:
+            src, dst = src.at[rows], dst.at[rows]
+        copy = pltpu.make_async_remote_copy(
+            src_ref=src,
+            dst_ref=dst,
+            send_sem=send_sem.at[places[key]],
+            recv_sem=recv_sem.at[places[key]],
+            device_id=target,
+            device_id_type=pl.DeviceIdType.MESH,
+        )
+        copy.start()
+        sent[key] = copy
+
+    keep = pltpu.make_async_copy(in_ref, out_ref.at[own_slot], own_sem)
+    keep.start()
+    for k in range(1, z_count):
+        send(("z", k), own_slot, others[k - 1], own=True)
+
+    def fan_out(k):
+        place = slot(zs[k], x, s)
+        send(("x", k), place, across, own=k == 0)
+        for d in range(1, sp_count):
+            send(("sp", k, d), place, device(z, x, c, to_sp[d]), own=k == 0)
+        send(("core", k), place, sibling, own=k == 0)
+
+    def relay(k):
+        sent[("x", k)].wait_recv()
+        place = slot(zs[k], 1 - x, s)
+        for d in range(1, sp_count):
+            send(("sp_a", k, d), place, device(z, x, c, to_sp[d]), upper)
+        send(("core_x", k), place, sibling)
+        for d in range(1, sp_count):
+            sent[("sp", k, d)].wait_recv()
+            place = slot(zs[k], x, from_sp[d])
+            send(("x_b", k, d), place, across, lower)
+            send(("core_sp", k, d), place, sibling)
+
+    def finish(k):
+        for d in range(1, sp_count):
+            place = slot(zs[k], 1 - x, from_sp[d])
+            sent[("sp_a", k, d)].wait_recv()
+            send(("core_a", k, d), place, sibling, upper)
+            sent[("x_b", k, d)].wait_recv()
+            send(("core_b", k, d), place, sibling, lower)
+
+    fan_out(0)
+    for k in range(1, z_count):
+        sent[("z", k)].wait_recv()
+        fan_out(k)
+        relay(k - 1)
+        if k > 1:
+            finish(k - 2)
+    relay(z_count - 1)
+    if z_count > 1:
+        finish(z_count - 2)
+    finish(z_count - 1)
+    keep.wait()
+    for key, copy in sent.items():
+        copy.wait_send()
+        if key[0].startswith("core"):
+            copy.wait_recv()
+
+
+def spread(shard, obs_count, sp_count, collective_id):
+    rows, cols = shard.shape
+    z_count = obs_count // 4
+    total = obs_count * sp_count
+    sems = len(spread_keys(z_count, sp_count))
+    gathered = pl.pallas_call(
+        functools.partial(spread_body, z_count, sp_count),
+        out_shape=jax.ShapeDtypeStruct((total, rows, cols), shard.dtype),
+        in_specs=[pl.BlockSpec(memory_space=pl.ANY)],
+        out_specs=pl.BlockSpec(memory_space=pl.ANY),
+        scratch_shapes=[
+            pltpu.SemaphoreType.DMA((sems,)),
+            pltpu.SemaphoreType.DMA((sems,)),
+            pltpu.SemaphoreType.DMA,
+        ],
+        compiler_params=pltpu.CompilerParams(collective_id=collective_id, has_side_effects=True),
+    )(shard)
+    return gathered.reshape(total * rows, cols)
+
+
 def on_device(descriptors, candidates, sparse_index, targets, regularizer):
     obs_count = lax.axis_size("obs")
     sp_count = lax.axis_size("sp")
@@ -232,7 +356,9 @@
     normalizer = 24.0 * descriptors.shape[0] * obs_count
 
     normed = unit_rows(descriptors)
-    table = lax.all_gather(unit_rows(candidates), "obs", axis=0, tiled=True)
+    piece = candidates.shape[0] // sp_count
+    own = lax.dynamic_slice_in_dim(candidates, sp_pos * piece, piece)
+    table = spread(unit_rows(own), obs_count, sp_count, 2)
     sparse = table.at[sparse_index].get(mode="promise_in_bounds")
 
     gram, sums = gram_call(
@@ -252,7 +378,7 @@
     scaled = jnp.where(
         on_diag, 0.0, part.astype(jnp.float32) * (rrow[:, None] / normalizer) * rwin[None, :]
     ).astype(jnp.bfloat16)
-    packed = lax.all_gather(scaled, ("obs", "sp"), axis=0, tiled=True)
+    packed = spread(scaled, obs_count, sp_count, 3)
 
     y = lax.dynamic_slice_in_dim(projected, col_start, tile)
     pos = jnp.stack([sp_pos, obs_pos]).astype(jnp.int32)

time: 439 us -> 385 us (0.88)
  waiting for transfers between devices: 293 us -> 90.8 us
  Pallas kernels: 91.7 us -> 239 us
    all_gather x2 -> x0, waiting for transfers between devices: 199 us -> none  [the longest x1 123 us: on_device(): packed = lax.all_gather(scaled, ('obs', 'sp'), axis=0, tiled=True)]
    pallas_call x0 -> x2, Pallas kernels: none -> 147 us  [spread(): pl.pallas_call(functools.partial(spread_body, z_count, sp_count), out_sha...]
  transfers between devices with their start and end apart: 3 -> 1, of which waited for: 3 -> 1; matrix products, arithmetic and copies ran while one was open for 2% -> 1% of each run, Pallas kernels for 3% -> 3%
where the time goes in v3:
time: 385 us; the launch traced here: 384 us
  Pallas kernels  239 us (62%)
  waiting for transfers between devices  90.8 us (24%)
  local copies, waits for them, and re-layouts  29.3 us (8%)
  between operations  14.1 us (4%)
  other arithmetic  10.7 us (3%)
    pallas_call x2, Pallas kernels, spread(): pl.pallas_call(functools.partial(spread_body, z_count, sp_count), out_sha...  147 us
    reduce_scatter x1, waiting for transfers between devices, on_device(): part = lax.psum_scatter(gram, 'obs', scatter_dimension=0, tiled=True)  90.8 us
    pallas_call x1, Pallas kernels, newton_call(): pl.pallas_call(functools.partial(newton_body, blocks, tile, share, sp_cou...  38.8 us
    pallas_call x1, Pallas kernels, gram_call(): pl.pallas_call(functools.partial(gram_body, blocks, tile, share, ext, mat...  31.4 us
    pallas_call x2, Pallas kernels, add_over_obs(): pl.pallas_call(functools.partial(add_body, count), out_shape=jax.ShapeDty...  22.4 us
    gather x1, local copies, waits for them, and re-layouts, on_device(): sparse = table.at[sparse_index].get(mode='promise_in_bounds')  21.9 us
  transfers between devices with their start and end apart: 1, of which 1 were waited for; matrix products, arithmetic and copies ran while one was open for 1% of the time, Pallas kernels for 3%

profile of v3, /device:TPU:0, one launch (start us, length us, event | category | flops | bytes accessed | tf_op | source)
XLA Modules:
  0.0 384.3 jit_solution(17997667597203393761)
XLA Ops:
  7.2 0.0 copy-start
  7.2 0.0 reduce-scatter.2.cloned.1.call-start
  7.2 1.2 fusion.2
  8.4 1.5 fusion
  9.9 0.7 fusion.4
  10.6 1.8 fusion.3.in_ref
  12.4 0.0 copy-done
  12.4 1.3 fusion.1.norm_ref
  13.7 50.5 %shard_map.68 = bf16[32,256,512]{2,1,0:T(8,128)(2,1)} custom-call(bf16[256,512]{1,0:T(8,128)(2,1)} %fusion.3.in_ref), custom_call_target="tpu_custom_call" | custom-call | tf_op jit(solution)/shard_map/pallas_call | solution.py:333
  64.2 0.0 copy-start.4
  64.2 21.9 %gather_fusion = bf16[4096,512]{1,0:T(8,128)(2,1)} fusion(bf16[8192,512]{1,0:T(8,128)(2,1)} %bitcast.14, s32[4096]{0:T(1024)S(1)} %fusion.4), kind=kCustom, calls=%fused_computation | custom fusion | bytes 8404992 | tf_op jit(solution)/shard_map/gather | solution.py:362
  86.1 0.0 copy-done.4
  86.1 0.6 broadcast_in_dim.16.tgt_ref
  86.7 31.4 %shard_map.69 = (bf16[4096,1152]{1,0:T(8,128)(2,1)}, f32[2,4096]{1,0:T(2,128)}) custom-call(s32[1]{0:T(128)} %bitcast.s_ref, bf16[1024,512]{1,0:T(8,128)(2,1)} %fusion.1.norm_ref, bf16[4096,512]{1,0:T(8,128)(2,1)} %gather_fusion, bf16[16,1024]{1,0:T(8,128)(2,1)} %broadcast_in_dim.16.tgt_ref), custom_call_target="tpu_custom_call" | custom-call | tf_op jit(solution)/shard_map/pallas_call | solution.py:61
  118.2 0.0 copy-start.2
  118.2 0.0 copy-start.3
  118.2 0.0 reduce-scatter.2.cloned.1.call-update
  118.2 0.7 copy-done.2
  118.9 0.6 reshape.47.in_ref
  119.6 13.2 %shard_map.70 = f32[64,128]{1,0:T(8,128)} custom-call(f32[64,128]{1,0:T(8,128)} %reshape.47.in_ref), custom_call_target="tpu_custom_call" | custom-call | flops 131072 | bytes 3276800 | tf_op jit(solution)/shard_map/pallas_call | solution.py:206
  132.7 0.0 copy-start.1
  132.7 0.0 copy-done.3
  132.8 0.8 fusion.5
  133.5 2.0 copy.7.rcol_ref
  135.5 0.0 copy-done.1
  135.5 0.1 dynamic_slice.15
  135.6 0.6 pad_add_fusion.pos_ref
  136.2 0.6 broadcast_multiply_fusion
  136.8 0.1 fusion.6
  136.9 90.8 %reduce-scatter.2.cloned.1.call-done = bf16[256,1152]{1,0:T(8,128)(2,1)} async-done(((bf16[4096,1152]{1,0:T(8,128)(2,1)}), bf16[256,1152]{1,0:T(8,128)(2,1)}) %reduce-scatter.2.cloned.1.call-update) | async-done | bytes 589840 | tf_op jit(solution)/shard_map/reduce_scatter | solution.py:368
  227.6 2.2 select_convert_fusion.in_ref
  229.8 96.2 %shard_map.71 = bf16[32,256,1152]{2,1,0:T(8,128)(2,1)} custom-call(bf16[256,1152]{1,0:T(8,128)(2,1)} %select_convert_fusion.in_ref), custom_call_target="tpu_custom_call" | custom-call | tf_op jit(solution)/shard_map/pallas_call | solution.py:333
  326.0 0.6 broadcast_in_dim.19.y_ref
  326.6 38.8 %shard_map.72 = (f32[2048,256]{1,0:T(8,128)}, f32[8,2048]{1,0:T(8,128)}) custom-call(s32[2]{0:T(128)} %pad_add_fusion.pos_ref, bf16[8192,1152]{1,0:T(8,128)(2,1)} %bitcast.15, f32[4096,1]{1,0:T(8,128)} %copy.7.rcol_ref, f32[1,256]{1,0:T(1,128)} %bitcast.19, f32[8,256]{1,0:T(8,128)} %broadcast_in_dim.19.y_ref), custom_call_target="tpu_custom_call" | custom-call | tf_op jit(solution)/shard_map/pallas_call | solution.py:146
  365.5 1.4 slice.13
  366.9 9.2 %shard_map.73 = f32[16,128]{1,0:T(8,128)} custom-call(f32[16,128]{1,0:T(8,128)} %bitcast.18), custom_call_target="tpu_custom_call" | custom-call | flops 32768 | bytes 819200 | tf_op jit(solution)/shard_map/pallas_call | solution.py:206
  376.1 1.3 copy.9
  (4 shorter events, 0.0 us)
Async XLA Ops:
  7.2 5.3 %copy-start = (bf16[1024,512]{1,0:T(8,128)(2,1)S(1)}, bf16[1024,512]{1,0:T(8,128)(2,1)}, u32[]{:S(2)}) copy-start(bf16[1024,512]{1,0:T(8,128)(2,1)} %param.5) | copy-start | bytes 3145732
  7.2 220.4 %reduce-scatter.2.cloned.1.call-start = ((), (), s32[]{:S(2)}) async-start(), calls=%async_computation.1 | async-start | bytes 10027008 | tf_op jit(solution)/shard_map/reduce_scatter | solution.py:368
  64.2 21.9 %copy-start.4 = (bf16[1024]{0:T(1024)(128)(2,1)S(1)}, bf16[1024]{0:T(1024)(128)(2,1)}, u32[]{:S(2)}) copy-start(bf16[1024]{0:T(1024)(128)(2,1)} %param.8) | copy-start | bytes 6148
  118.2 0.8 copy-start.2
  118.2 14.6 %copy-start.3 = (f32[4096]{0:T(1024)S(1)}, f32[4096]{0:T(1024)}, u32[]{:S(2)}) copy-start(f32[4096]{0:T(1024)} %param.9) | copy-start | bytes 49156
  132.7 2.8 copy-start.1
Sparse Core Ops, SparseCore 0:
  118.3 109.2 reduce-scatter.1

commit v4 on v3

--- a/solution.py
+++ b/solution.py
@@ -20,7 +20,9 @@
     )
 
 
-def gram_body(blocks, tile, share, ext, root, s_ref, norm_ref, sp_ref, tgt_ref, gram_ref, ws_ref, kext):
+def gram_body(
+    blocks, tile, share, first, ext, root, s_ref, norm_ref, sp_ref, tgt_ref, gram_ref, late_ref, ws_ref, kext
+):
     step = pl.program_id(0)
     width = blocks * tile
 
@@ -48,18 +50,20 @@
         j = step - blocks
         cols = pl.ds(pl.multiple_of(j * tile, tile), tile)
         window = pl.ds(pl.multiple_of(j * tile + s_ref[0] * share, LANES), share)
-        gram_ref[...] = lax.dot_general(
+        product = lax.dot_general(
             kext[:, cols], kext[:, window], (((0,), (0,)), ((), ())), preferred_element_type=jnp.float32
         ).astype(jnp.bfloat16)
-
-
-def gram_call(s_pos, normed, sparse, targets, blocks, tile, share, sp_count):
+        gram_ref[...] = product[:, :first]
+        late_ref[...] = product[:, first:]
+
+
+def gram_call(s_pos, normed, sparse, targets, blocks, tile, share, first, sp_count):
     rows, depth = normed.shape
     width = blocks * tile
     ext = -(-((blocks - 1) * tile + sp_count * share - width) // tile)
     last = blocks - 1
     return pl.pallas_call(
-        functools.partial(gram_body, blocks, tile, share, ext, math.sqrt(depth)),
+        functools.partial(gram_body, blocks, tile, share, first, ext, math.sqrt(depth)),
         grid_spec=pltpu.PrefetchScalarGridSpec(
             num_scalar_prefetch=1,
             grid=(2 * blocks,),
@@ -69,13 +73,15 @@
                 pl.BlockSpec((16, rows), lambda g, s: (0, 0)),
             ],
             out_specs=[
-                pl.BlockSpec((tile, share), lambda g, s: (jnp.maximum(g - blocks, 0), 0)),
+                pl.BlockSpec((tile, first), lambda g, s: (jnp.maximum(g - blocks, 0), 0)),
+                pl.BlockSpec((tile, share - first), lambda g, s: (jnp.maximum(g - blocks, 0), 0)),
                 pl.BlockSpec((2, tile), lambda g, s: (0, jnp.minimum(g, last))),
             ],
             scratch_shapes=[pltpu.VMEM((rows, width + ext * tile), jnp.bfloat16)],
         ),
         out_shape=[
-            jax.ShapeDtypeStruct((width, share), jnp.bfloat16),
+            jax.ShapeDtypeStruct((width, first), jnp.bfloat16),
+            jax.ShapeDtypeStruct((width, share - first), jnp.bfloat16),
             jax.ShapeDtypeStruct((2, width), jnp.float32),
         ],
         compiler_params=pltpu.CompilerParams(vmem_limit_bytes=VMEM_BYTES),
@@ -83,8 +89,8 @@
 
 
 def newton_body(
-    blocks, tile, share, sp_count, chunk, block_rows,
-    pos_ref, packed_ref, rcol_ref, rrow_ref, y_ref, inv_ref, w_ref, dense, prod,
+    blocks, tile, share, first, sp_count, chunk, block_rows,
+    pos_ref, packed_ref, late_ref, rcol_ref, rrow_ref, y_ref, inv_ref, w_ref, dense, prod,
 ):
     step = pl.program_id(0)
     width = blocks * tile
@@ -102,7 +108,8 @@
                     continue
                 col = lax.rem(step * tile + offset, width)
                 cols = pl.ds(pl.multiple_of(col, LANES), LANES)
-                block = packed_ref[s * tile : (s + 1) * tile, q * LANES : (q + 1) * LANES]
+                source, at = (packed_ref, q * LANES) if q * LANES < first else (late_ref, q * LANES - first)
+                block = source[s * tile : (s + 1) * tile, at : at + LANES]
                 dense[rows, cols] = block
                 if tile <= offset < half * tile:
                     dense[cols, rows] = block.T
@@ -137,19 +144,20 @@
         )
 
 
-def newton_call(pos, packed, root_recip, rrow, y, blocks, tile, share, sp_count):
+def newton_call(pos, packed, late, root_recip, rrow, y, blocks, tile, share, first, sp_count):
     width = blocks * tile
     block_rows = width // sp_count
     chunk = min(512, block_rows)
     grid = blocks + width // chunk + block_rows // chunk
     last = blocks - 1
     return pl.pallas_call(
-        functools.partial(newton_body, blocks, tile, share, sp_count, chunk, block_rows),
+        functools.partial(newton_body, blocks, tile, share, first, sp_count, chunk, block_rows),
         grid_spec=pltpu.PrefetchScalarGridSpec(
             num_scalar_prefetch=1,
             grid=(grid,),
             in_specs=[
-                pl.BlockSpec((sp_count * tile, share), lambda g, p: (jnp.minimum(g, last), 0)),
+                pl.BlockSpec((sp_count * tile, first), lambda g, p: (jnp.minimum(g, last), 0)),
+                pl.BlockSpec((sp_count * tile, share - first), lambda g, p: (jnp.minimum(g, last), 0)),
                 pl.BlockSpec((width, 1), lambda g, p: (0, 0)),
                 pl.BlockSpec((1, tile), lambda g, p: (0, 0)),
                 pl.BlockSpec((8, tile), lambda g, p: (0, 0)),
@@ -168,7 +176,7 @@
             jax.ShapeDtypeStruct((8, block_rows), jnp.float32),
         ],
         compiler_params=pltpu.CompilerParams(vmem_limit_bytes=VMEM_BYTES),
-    )(pos, packed, root_recip[:, None], rrow[None, :], jnp.broadcast_to(y[None, :], (8, tile)))
+    )(pos, packed, late, root_recip[:, None], rrow[None, :], jnp.broadcast_to(y[None, :], (8, tile)))
 
 
 def add_body(count, in_ref, out_ref, slots, send_sem, recv_sem):
@@ -340,6 +348,9 @@
             pltpu.SemaphoreType.DMA((sems,)),
             pltpu.SemaphoreType.DMA,
         ],
+        cost_estimate=pl.CostEstimate(
+            flops=0, bytes_accessed=16 * total * rows * cols, transcendentals=0
+        ),
         compiler_params=pltpu.CompilerParams(collective_id=collective_id, has_side_effects=True),
     )(shard)
     return gathered.reshape(total * rows, cols)
@@ -361,11 +372,13 @@
     table = spread(unit_rows(own), obs_count, sp_count, 2)
     sparse = table.at[sparse_index].get(mode="promise_in_bounds")
 
-    gram, sums = gram_call(
-        sp_pos[None].astype(jnp.int32), normed, sparse, targets, obs_count, tile, share, sp_count
+    first = -(-share // (2 * LANES)) * LANES
+    gram, late_gram, sums = gram_call(
+        sp_pos[None].astype(jnp.int32), normed, sparse, targets, obs_count, tile, share, first, sp_count
     )
     sums = add_over_obs(sums, obs_count, 0)
     part = lax.psum_scatter(gram, "obs", scatter_dimension=0, tiled=True)
+    late_part = lax.psum_scatter(late_gram, "obs", scatter_dimension=0, tiled=True)
 
     projected = sums[0] / math.sqrt(normalizer)
     root = lax.rsqrt(sums[1] / normalizer + regularizer)
@@ -375,15 +388,19 @@
     rwin = lax.dynamic_slice_in_dim(jnp.concatenate([root, root]), window_start, share)
     offset = sp_pos * share + lax.iota(jnp.int32, share)
     on_diag = lax.iota(jnp.int32, tile)[:, None] == offset[None, :]
-    scaled = jnp.where(
-        on_diag, 0.0, part.astype(jnp.float32) * (rrow[:, None] / normalizer) * rwin[None, :]
-    ).astype(jnp.bfloat16)
-    packed = spread(scaled, obs_count, sp_count, 3)
+    row_scale = rrow[:, None] / normalizer
+
+    def scale(block, cols):
+        scaled = block.astype(jnp.float32) * row_scale * rwin[None, cols]
+        return jnp.where(on_diag[:, cols], 0.0, scaled).astype(jnp.bfloat16)
+
+    packed = spread(scale(part, slice(0, first)), obs_count, sp_count, 3)
+    late = spread(scale(late_part, slice(first, share)), obs_count, sp_count, 4)
 
     y = lax.dynamic_slice_in_dim(projected, col_start, tile)
     pos = jnp.stack([sp_pos, obs_pos]).astype(jnp.int32)
     inverse_tile, part_w = newton_call(
-        pos, packed, root, rrow, y, obs_count, tile, share, sp_count
+        pos, packed, late, root, rrow, y, obs_count, tile, share, first, sp_count
     )
     return inverse_tile, add_over_obs(part_w[0], obs_count, 1)
 

time: 385 us -> 398 us (1.034)
  Pallas kernels: 239 us -> 255 us
  waiting for transfers between devices: 90.8 us -> 84.5 us
    reduce_scatter x1, waiting for transfers between devices: 90.8 us -> 32.9 us  [on_device(): part = lax.psum_scatter(gram, 'obs', scatter_dimension=0, tiled=True)]
    reduce_scatter x0 -> x1, waiting for transfers between devices: none -> 51 us  [on_device(): lax.psum_scatter(late_gram, 'obs', scatter_dimension=0, tiled=True)]
    pallas_call x2 -> x3, Pallas kernels: 147 us -> 163 us  [spread(): pl.pallas_call(functools.partial(spread_body, z_count, sp_count), out_sha...]
  transfers between devices with their start and end apart: 1 -> 2, of which waited for: 1 -> 2; matrix products, arithmetic and copies ran while one was open for 1% -> 2% of each run, Pallas kernels for 3% -> 18%
where the time goes in v4:
time: 398 us; the launch traced here: 396 us
  Pallas kernels  255 us (64%)
  waiting for transfers between devices  84.5 us (21%)
  local copies, waits for them, and re-layouts  28.6 us (7%)
  other arithmetic  14.3 us (4%)
  between operations  14.2 us (4%)
    pallas_call x3, Pallas kernels, spread(): pl.pallas_call(functools.partial(spread_body, z_count, sp_count), out_sha...  163 us
    reduce_scatter x1, waiting for transfers between devices, on_device(): lax.psum_scatter(late_gram, 'obs', scatter_dimension=0, tiled=True)  51 us
    pallas_call x1, Pallas kernels, newton_call(): pl.pallas_call(functools.partial(newton_body, blocks, tile, share, first,...  38.7 us
    reduce_scatter x1, waiting for transfers between devices, on_device(): part = lax.psum_scatter(gram, 'obs', scatter_dimension=0, tiled=True)  32.9 us
    pallas_call x1, Pallas kernels, gram_call(): pl.pallas_call(functools.partial(gram_body, blocks, tile, share, first, e...  31.4 us
    gather x1, local copies, waits for them, and re-layouts, on_device(): sparse = table.at[sparse_index].get(mode='promise_in_bounds')  21.9 us
    pallas_call x2, Pallas kernels, add_over_obs(): pl.pallas_call(functools.partial(add_body, count), out_shape=jax.ShapeDty...  21.5 us
  transfers between devices with their start and end apart: 2, of which 2 were waited for; matrix products, arithmetic and copies ran while one was open for 2% of the time, Pallas kernels for 18%

profile of v4, /device:TPU:0, one launch (start us, length us, event | category | flops | bytes accessed | tf_op | source)
XLA Modules:
  0.0 396.3 jit_solution(14258042072365121692)
XLA Ops:
  7.2 0.0 reduce-scatter.5.cloned.1.call-start
  7.2 1.1 fusion.2
  8.3 1.5 fusion
  9.8 0.7 fusion.4
  10.6 1.8 fusion.3.in_ref
  12.3 2.5 fusion.1.norm_ref
  14.8 50.5 %shard_map.68 = bf16[32,256,512]{2,1,0:T(8,128)(2,1)} custom-call(bf16[256,512]{1,0:T(8,128)(2,1)} %fusion.3.in_ref), custom_call_target="tpu_custom_call" | custom-call | bytes 67108864 | tf_op jit(solution)/shard_map/pallas_call | solution.py:341
  65.3 0.0 copy-start.2
  65.3 21.9 %gather_fusion = bf16[4096,512]{1,0:T(8,128)(2,1)} fusion(bf16[8192,512]{1,0:T(8,128)(2,1)} %bitcast.15, s32[4096]{0:T(1024)S(1)} %fusion.4), kind=kCustom, calls=%fused_computation | custom fusion | bytes 8404992 | tf_op jit(solution)/shard_map/gather | solution.py:373
  87.3 0.0 copy-done.2
  87.3 0.6 broadcast_in_dim.20.tgt_ref
  87.9 31.4 %shard_map.69 = (bf16[4096,640]{1,0:T(8,128)(2,1)}, bf16[4096,512]{1,0:T(8,128)(2,1)}, f32[2,4096]{1,0:T(2,128)}) custom-call(s32[1]{0:T(128)} %bitcast.s_ref, bf16[1024,512]{1,0:T(8,128)(2,1)} %fusion.1.norm_ref, bf16[4096,512]{1,0:T(8,128)(2,1)} %gather_fusion, bf16[16,1024]{1,0:T(8,128)(2,1)} %broadcast_in_dim.20.tgt_ref), custom_call_target="tpu_custom_call" | custom-call | tf_op jit(solution)/shard_map/pallas_call | solution.py:65
  119.3 0.0 copy-start
  119.3 0.0 copy-start.1
  119.3 0.0 reduce-scatter.5.cloned.1.call-update
  119.3 0.0 reduce-scatter.3.cloned.1.call-start
  119.4 0.7 reduce-scatter.3.cloned.1.call-update
  120.1 0.0 copy-done
  120.1 0.6 reshape.51.in_ref
  120.8 13.2 %shard_map.70 = f32[64,128]{1,0:T(8,128)} custom-call(f32[64,128]{1,0:T(8,128)} %reshape.51.in_ref), custom_call_target="tpu_custom_call" | custom-call | flops 131072 | bytes 3276800 | tf_op jit(solution)/shard_map/pallas_call | solution.py:214
  133.9 0.0 copy-done.1
  134.0 0.7 fusion.5
  134.7 0.1 fusion.6
  134.8 2.0 copy.7.rcol_ref
  136.7 0.7 multiply_bitcast_fusion
  137.5 0.1 dynamic_slice.15
  137.5 0.6 pad_add_fusion.pos_ref
  138.1 0.6 broadcast_multiply_fusion
  138.8 0.2 iota_compare_fusion
  138.9 51.0 %reduce-scatter.5.cloned.1.call-done = bf16[256,512]{1,0:T(8,128)(2,1)} async-done(((bf16[4096,512]{1,0:T(8,128)(2,1)}), bf16[256,512]{1,0:T(8,128)(2,1)}) %reduce-scatter.5.cloned.1.call-update) | async-done | bytes 262160 | tf_op jit(solution)/shard_map/reduce_scatter | solution.py:381
  189.9 1.8 select_convert_fusion.1.in_ref
  191.7 56.7 %shard_map.72 = bf16[32,256,512]{2,1,0:T(8,128)(2,1)} custom-call(bf16[256,512]{1,0:T(8,128)(2,1)} %select_convert_fusion.1.in_ref), custom_call_target="tpu_custom_call" | custom-call | bytes 67108864 | tf_op jit(solution)/shard_map/pallas_call | solution.py:341
  248.5 32.9 %reduce-scatter.3.cloned.1.call-done = bf16[256,640]{1,0:T(8,128)(2,1)} async-done(((bf16[4096,640]{1,0:T(8,128)(2,1)}), bf16[256,640]{1,0:T(8,128)(2,1)}) %reduce-scatter.3.cloned.1.call-update) | async-done | bytes 327696 | tf_op jit(solution)/shard_map/reduce_scatter | solution.py:380
  281.4 1.9 select_convert_fusion.in_ref
  283.3 55.8 %shard_map.71 = bf16[32,256,640]{2,1,0:T(8,128)(2,1)} custom-call(bf16[256,640]{1,0:T(8,128)(2,1)} %select_convert_fusion.in_ref), custom_call_target="tpu_custom_call" | custom-call | bytes 83886080 | tf_op jit(solution)/shard_map/pallas_call | solution.py:341
  339.0 0.6 broadcast_in_dim.43.y_ref
  339.6 38.7 %shard_map.73 = (f32[2048,256]{1,0:T(8,128)}, f32[8,2048]{1,0:T(8,128)}) custom-call(s32[2]{0:T(128)} %pad_add_fusion.pos_ref, bf16[8192,640]{1,0:T(8,128)(2,1)} %bitcast.16, bf16[8192,512]{1,0:T(8,128)(2,1)} %bitcast.17, f32[4096,1]{1,0:T(8,128)} %copy.7.rcol_ref, f32[1,256]{1,0:T(1,128)} %bitcast.21, f32[8,256]{1,0:T(8,128)} %broadcast_in_dim.43.y_ref), custom_call_target="tpu_custom_call" | custom-call | tf_op jit(solution)/shard_map/pallas_call | solution.py:153
  378.3 1.4 slice.29
  379.8 8.4 %shard_map.74 = f32[16,128]{1,0:T(8,128)} custom-call(f32[16,128]{1,0:T(8,128)} %bitcast.20), custom_call_target="tpu_custom_call" | custom-call | flops 32768 | bytes 819200 | tf_op jit(solution)/shard_map/pallas_call | solution.py:214
  388.1 1.3 copy.9
  (5 shorter events, 0.0 us)
Async XLA Ops:
  7.2 182.7 %reduce-scatter.5.cloned.1.call-start = ((), (), s32[]{:S(2)}) async-start(), calls=%async_computation.3 | async-start | bytes 4456448 | tf_op jit(solution)/shard_map/reduce_scatter | solution.py:381
  65.3 22.0 %copy-start.2 = (bf16[1024]{0:T(1024)(128)(2,1)S(1)}, bf16[1024]{0:T(1024)(128)(2,1)}, u32[]{:S(2)}) copy-start(bf16[1024]{0:T(1024)(128)(2,1)} %param.8) | copy-start | bytes 6148
  119.3 0.8 copy-start
  119.3 14.6 %copy-start.1 = (f32[4096]{0:T(1024)S(1)}, f32[4096]{0:T(1024)}, u32[]{:S(2)}) copy-start(f32[4096]{0:T(1024)} %param.9) | copy-start | bytes 49156
  119.3 162.0 %reduce-scatter.3.cloned.1.call-start = ((), (), s32[]{:S(2)}) async-start(), calls=%async_computation.2 | async-start | bytes 5570560 | tf_op jit(solution)/shard_map/reduce_scatter | solution.py:380
Sparse Core Ops, SparseCore 0:
  119.5 70.3 reduce-scatter.4
  194.3 87.0 reduce-scatter.2
